TPU v7x, 32 devices: a whole 2x2x4 slice. The times are simulated.
32 devices in a mesh: seq: 4 (over y, x), grp: 8 (over z, core).
Axes of the slice: x: 2, y: 2, z: 4, core: 2. Of those that a mesh axis runs over, the one named last changes fastest.
Arguments:
- tokens: bfloat16 [16384, 768], P(('grp', 'seq')), may hold values from -6 to 6
- cotangent: bfloat16 [16384, 768], P(('grp', 'seq')), may hold values from -6 to 6
- seq_len: int32 [8], P('grp'), may hold values from 1024 to 2048, as said below
- weight_mats: bfloat16 [768, 9280], replicated
- weight_vecs: bfloat16 [768, 13], replicated
- master_mats: float32 [768, 9280], P('grp'), may hold values from -0.21875 to 0.21875
- master_vecs: float32 [768, 13], P('grp'), may hold values from -3 to 3
- moment_mats: float32 [768, 9280], P('grp'), may hold values from -384 to 384
- moment_vecs: float32 [768, 13], P('grp'), may hold values from -384 to 384
- square_mats: float32 [768, 9280], P('grp'), may hold values from 819.2 to 32768
- square_vecs: float32 [768, 13], P('grp'), may hold values from 819.2 to 32768
- average_mats: float32 [768, 9280], P('grp'), may hold values from -0.21875 to 0.21875
- average_vecs: float32 [768, 13], P('grp'), may hold values from -3 to 3
Outputs:
- block_output: bfloat16 [16384, 768], P(('grp', 'seq'))
- input_grad: bfloat16 [16384, 768], P(('grp', 'seq'))
- grad_mats: float32 [768, 9280], P('grp')
- grad_vecs: float32 [768, 13], P('grp')
- master_mats_new: float32 [768, 9280], P('grp')
- master_vecs_new: float32 [768, 13], P('grp')
- moment_mats_new: float32 [768, 9280], P('grp')
- moment_vecs_new: float32 [768, 13], P('grp')
- square_mats_new: float32 [768, 9280], P('grp')
- square_vecs_new: float32 [768, 13], P('grp')
- average_mats_new: float32 [768, 9280], P('grp')
- average_vecs_new: float32 [768, 13], P('grp')
- copy_mats: bfloat16 [768, 9280], P('grp')
- copy_vecs: bfloat16 [768, 13], P('grp')
Inputs may be any that keep to these rules, and one draw needn't show every extreme that they name: Each group's sequences all have the length seq_len of that group; both values 2 * 512 and 2048 occur in every draw.
All inputs are finite; a program needn't handle non-finite values.
Results may differ from a plain program's by a relative error of at most 0.018.
Values may be sent and summed in bfloat16 or wider, within the bound.
No kernel may reach another device: no remote copies, remote signals or barrier semaphores. Data moves between devices by JAX's collectives and lax.ppermute only.
A program may use at most 192 MiB of HBM per device.

v0:
```python
from functools import partial
import jax
import jax.numpy as jnp
from jax import lax
from jax.sharding import PartitionSpec as P

D = 768
HEADS = 12
HD = 64
FF = 3072
norm_eps = 1e-05
adam_eps = 1e-08
beta_first = 0.5
beta_second = 0.5
learn_rate = 0.01
vector_rate = 0.06
decay_rate = 0.1
average_keep = 0.9
highest = lax.Precision.HIGHEST
careful_level = lax.Precision.HIGH


def contract_rows(left, right):
    return lax.dot_general(
        left, right, (((0,), (0,)), ((), ())), preferred_element_type=jnp.float32
    )


def contract_cols(left, right):
    return lax.dot_general(
        left, right, (((1,), (1,)), ((), ())), preferred_element_type=jnp.float32
    )


def precise(left, right):
    return jnp.dot(left, right, preferred_element_type=jnp.float32, precision=careful_level)


def norm_rows(values, gain, shift):
    average = jnp.mean(values, axis=1, keepdims=True)
    centered = values - average
    variance = jnp.mean(centered * centered, axis=1, keepdims=True)
    return centered * lax.rsqrt(variance + norm_eps) * gain + shift


def norm_back(values, gain, upstream):
    average = jnp.mean(values, axis=1, keepdims=True)
    centered = values - average
    variance = jnp.mean(centered * centered, axis=1, keepdims=True)
    inverse = lax.rsqrt(variance + norm_eps)
    normed = centered * inverse
    d_gain = jnp.sum(upstream * normed, axis=0)
    d_shift = jnp.sum(upstream, axis=0)
    d_normed = upstream * gain
    d_values = inverse * (
        d_normed
        - jnp.mean(d_normed, axis=1, keepdims=True)
        - normed * jnp.mean(d_normed * normed, axis=1, keepdims=True)
    )
    return (d_values, d_gain, d_shift)


def feature_map(values, hedge_map):
    count = values.shape[0]
    per_head = values.reshape(count, HEADS, HD)
    scores = jnp.einsum("nhi,hij->nhj", per_head, hedge_map, precision=highest)
    return jnp.concatenate(
        [jax.nn.softmax(scores, axis=-1), jax.nn.softmax(-scores, axis=-1)], axis=-1
    )


def adam_step(grad, master, first, second, rate):
    new_first = beta_first * first + (1.0 - beta_first) * grad
    new_second = beta_second * second + (1.0 - beta_second) * grad * grad
    new_master = master - rate * (
        new_first / (jnp.sqrt(new_second) + adam_eps) + decay_rate * master
    )
    return (new_master, new_first, new_second)


def on_device(
    tokens,
    cotangent,
    seq_len,
    weight_mats,
    weight_vecs,
    master_mats,
    master_vecs,
    moment_mats,
    moment_vecs,
    square_mats,
    square_vecs,
    average_mats,
    average_vecs,
):
    rows = tokens.shape[0]
    my_start = lax.axis_index("seq") * rows
    seq_length = seq_len[0]
    starts = (my_start % seq_length == 0).astype(jnp.float32)
    continued = 1.0 - starts
    w_qkv = weight_mats[:, : 3 * D]
    w_proj = weight_mats[:, 3 * D : 4 * D]
    w_fc = weight_mats[:, 4 * D : 4 * D + FF]
    w_down = weight_mats[:, 4 * D + FF : 4 * D + 2 * FF]
    hedge_map = weight_mats[:, 4 * D + 2 * FF :].astype(jnp.float32).reshape(HEADS, HD, HD)
    vec_all = weight_vecs.astype(jnp.float32)
    gain_one = vec_all[:, 0]
    gain_two = vec_all[:, 2]
    bias_qkv = vec_all[:, 6:9].T.reshape(3 * D)
    bias_fc = vec_all[:, 9:].T.reshape(FF)
    line_index = jnp.arange(rows, dtype=jnp.int32)
    causal = (line_index[:, None] >= line_index[None, :]).astype(jnp.float32)
    inputs = tokens.astype(jnp.float32)
    normed_low = norm_rows(inputs, gain_one, vec_all[:, 1]).astype(jnp.bfloat16)
    projected = jnp.dot(normed_low, w_qkv, preferred_element_type=jnp.float32) + bias_qkv
    queries = projected[:, :D]
    keys = projected[:, D : 2 * D]
    values_low = projected[:, 2 * D :].astype(jnp.bfloat16)
    query_full, query_back = jax.vjp(feature_map, queries, hedge_map)
    key_full, key_back = jax.vjp(feature_map, keys, hedge_map)
    query_feat = query_full.astype(jnp.bfloat16)
    key_feat = key_full.astype(jnp.bfloat16)
    value_heads = values_low.reshape(rows, HEADS, HD)
    gath_keys, gath_values = (
        lax.all_gather(key_feat.reshape(rows, 2 * D), "seq", axis=0, tiled=True),
        lax.all_gather(values_low, "seq", axis=0, tiled=True),
    )
    positions = jnp.arange(gath_keys.shape[0], dtype=jnp.int32)
    keep_rows = (
        (positions < my_start) & (positions // seq_length == my_start // seq_length)
    ).astype(jnp.bfloat16)
    kept_keys = (gath_keys * keep_rows[:, None]).reshape(-1, HEADS, 2 * HD)
    state_in = jnp.einsum(
        "nhf,nhd->hfd",
        kept_keys,
        gath_values.reshape(-1, HEADS, HD),
        preferred_element_type=jnp.float32,
    )
    total_in = jnp.sum(kept_keys, axis=0, dtype=jnp.float32)
    query_heads = jnp.transpose(query_feat, (1, 0, 2))
    key_heads = jnp.transpose(key_feat, (1, 0, 2))
    value_major = jnp.transpose(value_heads, (1, 0, 2))

    def attend(parts):
        query_part, key_part, value_part, state, total = parts
        query_wide = query_part.astype(jnp.float32)
        weights = jnp.dot(query_part, key_part.T, preferred_element_type=jnp.float32) * causal
        numer = precise(weights, value_part.astype(jnp.float32)) + precise(query_wide, state)
        denom = jnp.sum(weights, axis=1) + precise(query_wide, total)
        return (numer / denom[:, None], denom)

    head_outs, denoms = lax.map(attend, (query_heads, key_heads, value_major, state_in, total_in))
    mixed_low = jnp.transpose(head_outs, (1, 0, 2)).reshape(rows, D).astype(jnp.bfloat16)
    attn_out = jnp.dot(mixed_low, w_proj, preferred_element_type=jnp.float32) + vec_all[:, 4]
    resid = inputs + attn_out
    normed_two_low = norm_rows(resid, gain_two, vec_all[:, 3]).astype(jnp.bfloat16)
    hidden_pre = jnp.dot(normed_two_low, w_fc, preferred_element_type=jnp.float32) + bias_fc
    hidden_act, gelu_back = jax.vjp(partial(jax.nn.gelu, approximate=True), hidden_pre)
    hidden_low = hidden_act.astype(jnp.bfloat16)
    result = resid + contract_cols(hidden_low, w_down) + vec_all[:, 5]
    block_output = result.astype(jnp.bfloat16)
    grad_out = cotangent.astype(jnp.float32)
    d_down = contract_rows(cotangent, hidden_low)
    d_bias_down = jnp.sum(grad_out, axis=0)
    d_hidden = jnp.dot(cotangent, w_down, preferred_element_type=jnp.float32)
    d_pre_low = gelu_back(d_hidden)[0].astype(jnp.bfloat16)
    d_fc = contract_rows(normed_two_low, d_pre_low)
    d_bias_fc = jnp.sum(d_pre_low.astype(jnp.float32), axis=0)
    d_normed_two = contract_cols(d_pre_low, w_fc)
    d_resid_norm, d_gain_two, d_shift_two = norm_back(resid, gain_two, d_normed_two)
    d_resid = grad_out + d_resid_norm
    d_attn_low = d_resid.astype(jnp.bfloat16)
    d_bias_proj = jnp.sum(d_attn_low.astype(jnp.float32), axis=0)
    d_proj = contract_rows(mixed_low, d_attn_low)
    d_mixed_low = lax.optimization_barrier(contract_cols(d_attn_low, w_proj).astype(jnp.bfloat16))
    d_mixed = jnp.transpose(d_mixed_low.astype(jnp.float32).reshape(rows, HEADS, HD), (1, 0, 2))

    def attend_back(parts):
        query_part, key_part, value_part, state, total, outs, denom, upstream = parts
        query_wide = query_part.astype(jnp.float32)
        key_wide = key_part.astype(jnp.float32)
        weights = jnp.dot(query_part, key_part.T, preferred_element_type=jnp.float32) * causal
        ratio = upstream / denom[:, None]
        offset = -jnp.sum(upstream * outs, axis=1) / denom
        d_weights = (precise(ratio, value_part.astype(jnp.float32).T) + offset[:, None]) * causal
        d_query = (
            precise(d_weights, key_wide)
            + precise(ratio, state.T)
            + offset[:, None] * total[None, :]
        )
        d_key = precise(d_weights.T, query_wide)
        d_value = precise(weights.T, ratio)
        back_state = precise(query_wide.T, ratio) * continued
        back_total = precise(offset, query_wide) * continued
        return (d_query, d_key, d_value, back_state, back_total)

    d_query_h, d_key_h, d_value_h, back_state, back_total = lax.map(
        attend_back,
        (query_heads, key_heads, value_major, state_in, total_in, head_outs, denoms, d_mixed),
    )
    count = rows * lax.axis_size("seq")
    keys_part = gath_keys.astype(jnp.float32).reshape(count, HEADS, 2 * HD)
    vals_part = gath_values.astype(jnp.float32).reshape(count, HEADS, HD)
    keep_part = keep_rows.astype(jnp.float32)
    d_keys_part = (
        jnp.einsum("nhd,hfd->nhf", vals_part, back_state, precision=careful_level)
        + back_total[None]
    ) * keep_part[:, None, None]
    d_vals_part = (
        jnp.einsum("nhf,hfd->nhd", keys_part, back_state, precision=careful_level)
        * keep_part[:, None, None]
    )
    remote = lax.psum_scatter(
        jnp.concatenate(
            [d_keys_part.reshape(count, 2 * D), d_vals_part.reshape(count, D)], axis=1
        ).astype(jnp.bfloat16),
        "seq",
        scatter_dimension=0,
        tiled=True,
    ).astype(jnp.float32)
    d_key_extra = remote[:, : 2 * D].reshape(rows, HEADS, 2 * HD)
    d_value_extra = remote[:, 2 * D :].reshape(rows, HEADS, HD)
    d_query_all = jnp.transpose(d_query_h, (1, 0, 2))
    d_key_all = jnp.transpose(d_key_h, (1, 0, 2)) + d_key_extra
    d_value_all = jnp.transpose(d_value_h, (1, 0, 2)) + d_value_extra
    d_queries, d_map_query = query_back(d_query_all)
    d_keys, d_map_key = key_back(d_key_all)
    d_proj_low = jnp.concatenate([d_queries, d_keys, d_value_all.reshape(rows, D)], axis=1).astype(
        jnp.bfloat16
    )
    d_qkv = contract_rows(normed_low, d_proj_low)
    d_bias_qkv = jnp.sum(d_proj_low.astype(jnp.float32), axis=0)
    d_normed_one = contract_cols(d_proj_low, w_qkv)
    d_input_norm, d_gain_one, d_shift_one = norm_back(inputs, gain_one, d_normed_one)
    input_grad = (d_resid + d_input_norm).astype(jnp.bfloat16)
    grad_mats = jnp.concatenate(
        [d_qkv, d_proj, d_fc, d_down, (d_map_query + d_map_key).reshape(D, HD)], axis=1
    )
    grad_vecs = jnp.concatenate(
        [
            jnp.stack(
                [d_gain_one, d_shift_one, d_gain_two, d_shift_two, d_bias_proj, d_bias_down], axis=1
            ),
            d_bias_qkv.reshape(3, D).T,
            d_bias_fc.reshape(FF // D, D).T,
        ],
        axis=1,
    )
    owned_mats, owned_vecs = (
        lax.psum_scatter(grad_mats, "grp", scatter_dimension=0, tiled=True),
        lax.psum_scatter(grad_vecs, "grp", scatter_dimension=0, tiled=True),
    )
    grad_mats_own, grad_vecs_own = (
        lax.psum(owned_mats.astype(jnp.bfloat16), "seq").astype(jnp.float32),
        lax.psum(owned_vecs.astype(jnp.bfloat16), "seq").astype(jnp.float32),
    )
    new_mats, new_first_m, new_second_m = adam_step(
        grad_mats_own, master_mats, moment_mats, square_mats, learn_rate
    )
    new_vecs, new_first_v, new_second_v = adam_step(
        grad_vecs_own, master_vecs, moment_vecs, square_vecs, vector_rate
    )
    new_avg_m = average_keep * average_mats + (1.0 - average_keep) * new_mats
    new_avg_v = average_keep * average_vecs + (1.0 - average_keep) * new_vecs
    return (
        block_output,
        input_grad,
        grad_mats_own,
        grad_vecs_own,
        new_mats,
        new_vecs,
        new_first_m,
        new_first_v,
        new_second_m,
        new_second_v,
        new_avg_m,
        new_avg_v,
        new_mats.astype(jnp.bfloat16),
        new_vecs.astype(jnp.bfloat16),
    )


def solution(mesh):
    in_specs = (
        P(("grp", "seq"), None),
        P(("grp", "seq"), None),
        P("grp"),
        P(),
        P(),
        P("grp", None),
        P("grp", None),
        P("grp", None),
        P("grp", None),
        P("grp", None),
        P("grp", None),
        P("grp", None),
        P("grp", None),
    )
    out_specs = (
        P(("grp", "seq"), None),
        P(("grp", "seq"), None),
        P("grp", None),
        P("grp", None),
        P("grp", None),
        P("grp", None),
        P("grp", None),
        P("grp", None),
        P("grp", None),
        P("grp", None),
        P("grp", None),
        P("grp", None),
        P("grp", None),
        P("grp", None),
    )
    return jax.shard_map(
        on_device, mesh=mesh, in_specs=in_specs, out_specs=out_specs, check_vma=False
    )
```

profile of v0, /device:TPU:0, one launch (start us, length us, event | category | flops | bytes accessed | tf_op | source)
XLA Modules:
  0.0 1010.2 jit_solution(10283826518961896790)
XLA Ops:
  11.6 4.2 convolution_add_fusion.3
  19.1 3.3 fusion.162
  25.0 2.4 fusion.165
  45.7 3.1 copy.80
  50.2 2.6 copy.81
  53.0 12.7 %all-gather.5.cloned.1.call-done = bf16[2048,768]{1,0:T(8,128)(2,1)} async-done(((bf16[512,768]{1,0:T(8,128)(2,1)}), bf16[2048,768]{1,0:T(8,128)(2,1)}) %all-gather.5.cloned.1.call-update) | async-done | bytes 3145744 | tf_op jit(solution)/shard_map/all_gather | solution.py:126
  65.8 4.6 copy.78
  70.4 67.8 %all-gather.3.cloned.1.call-done = bf16[2048,1536]{0,1:T(8,128)(2,1)} async-done(((bf16[512,1536]{0,1:T(8,128)(2,1)}), bf16[2048,1536]{0,1:T(8,128)(2,1)}) %all-gather.3.cloned.1.call-update) | async-done | bytes 6291472 | tf_op jit(solution)/shard_map/all_gather | solution.py:125
  138.2 5.0 convert_reduce_fusion
  146.4 81.3 %while.33 = (s32[]{:T(128)}, f32[12,512,64]{1,2,0:T(8,128)}, f32[12,512]{1,0:T(8,128)}, bf16[12,512,128]{2,1,0:T(8,128)(2,1)}, bf16[12,512,128]{2,1,0:T(8,128)(2...) while((s32[]{:T(128)}, f32[12,512,64]{1,2,0:T(8,128)}, ...), condition=%wide.region_13.14_spmd.clone, body=%wide.region_11.13_spmd.clone.sunk | while | flops 194183168 | bytes 3231861 | solution.py:152
  229.5 2.4 fusion.167
  232.4 5.0 fusion.85
  237.4 11.5 %convert_reduce_fusion.1 = (f32[3072]{0:T(1024)}, bf16[512,3072]{1,0:T(8,128)(2,1)S(1)}) fusion(f32[512,3072]{1,0:T(8,128)S(1)} %fusion.85, f32[3072]{0:T(1024)S(1)} %add.216, bf16[512,768]{1,0:T(8,128)(2,1)S(1)} %copy-done.40, bf16[768,9280]{0,1:T(8,128)(2,1)} %param.20), kind=kOutput, calls=%fused_computation.105 | convolution fusion | flops 2452091904 | bytes 14966784 | tf_op jit(solution)/shard_map/dot_general | solution.py:165
  249.0 3.5 multiply_reduce_fusion
  258.5 202.7 %while.34 = (s32[]{:T(128)}, f32[12,512,128]{1,2,0:T(8,128)}, f32[12,512,128]{1,2,0:T(8,128)}, f32[12,512,64]{1,2,0:T(8,128)}, f32[12,128,64]{1,2,0:T(8,128)}, /...) while((s32[]{:T(128)}, f32[12,512,128]{1,2,0:T(8,128)}, ...), condition=%wide.region_20.21_spmd.clone.clone, body=%wide.region_18.20_spmd.clone.clone.sunk | while | flops 723526784 | bytes 10363109 | solution.py:197
  461.3 5.1 multiply_convert_fusion.1
  466.4 5.4 multiply_convert_fusion
  471.8 11.6 %pad_maximum_fusion = bf16[2048,2304]{0,1:T(8,128)(2,1)} fusion(bf16[2048,768]{0,1:T(8,128)(2,1)S(1)} %bitcast.307, bf16[2048,1536]{0,1:T(8,128)(2,1)S(1)} %bitcast.302), kind=kLoop, calls=%fused_computation.92 | loop fusion | flops 18874368 | bytes 18874368 | tf_op jit(solution)/shard_map/concatenate | solution.py:214
  484.8 3.4 multiply_reduce_fusion.4
  491.5 87.1 %reduce-scatter.6.cloned.1.call-done = bf16[512,2304]{0,1:T(8,128)(2,1)} async-done(((bf16[2048,2304]{0,1:T(8,128)(2,1)}), bf16[512,2304]{0,1:T(8,128)(2,1)}) %reduce-scatter.6.cloned.1.call-update) | async-done | bytes 2359312 | tf_op jit(solution)/shard_map/reduce_scatter | solution.py:213
  592.2 5.4 convolution_dynamic-update-slice_fusion
  600.0 5.5 convolution_dynamic-update-slice_fusion.1
  605.5 5.5 bitcast_dynamic-update-slice_fusion
  614.4 6.0 fusion.110
  621.8 270.7 %reduce-scatter.8.cloned.1.call-done = f32[96,9280]{1,0:T(8,128)} async-done(((f32[768,9280]{1,0:T(8,128)}), f32[96,9280]{1,0:T(8,128)}) %reduce-scatter.8.cloned.1.call-update) | async-done | bytes 3563536 | tf_op jit(solution)/shard_map/reduce_scatter | solution.py:250
  892.5 3.4 convert_element_type.146
  896.6 9.6 add_convert_fusion
  907.7 16.4 %reduce-scatter.10.cloned.1.call-done = f32[96,13]{1,0:T(8,128)} async-done(((f32[768,13]{1,0:T(8,128)}), f32[96,13]{1,0:T(8,128)}) %reduce-scatter.10.cloned.1.call-update) | async-done | bytes 5008
  925.0 10.0 psum.15
  936.3 54.8 %all-reduce.2.cloned.1.call-done = bf16[96,9280]{1,0:T(8,128)(2,1)} async-done(((bf16[96,9280]{1,0:T(8,128)(2,1)}), bf16[96,9280]{1,0:T(8,128)(2,1)}) %all-reduce.2.cloned.1.call-update) | async-done | bytes 1781776 | tf_op jit(solution)/shard_map/psum | solution.py:254
  991.1 8.9 fusion.158
  1000.1 2.8 multiply_add_fusion.1
  (577 shorter events, 353.1 us)
Async XLA Ops:
  7.2 58.6 %all-gather.5.cloned.1.call-start = ((), (), s32[]{:S(2)}) async-start(), calls=%async_computation.4 | async-start | bytes 3932160 | tf_op jit(solution)/shard_map/all_gather | solution.py:126
  8.7 7.1 copy-start.53
  8.7 7.1 copy-start.71
  8.7 223.7 %copy-start.69 = (f32[768]{0:T(1024)}, f32[768]{0:T(1024)S(1)}, u32[]{:S(2)}) copy-start(f32[768]{0:T(1024)S(1)} %get-tuple-element.327) | copy-start | bytes 9220
  8.7 243.8 %copy-start.51 = (f32[768]{0:T(1024)}, f32[768]{0:T(1024)S(1)}, u32[]{:S(2)}) copy-start(f32[768]{0:T(1024)S(1)} %get-tuple-element.325) | copy-start | bytes 9220
  10.0 5.7 copy-start.45
  18.9 119.3 %all-gather.3.cloned.1.call-start = ((), (), s32[]{:S(2)}) async-start(), calls=%async_computation.3 | async-start | bytes 7864320 | tf_op jit(solution)/shard_map/all_gather | solution.py:125
  19.1 18.3 %copy-start.30 = (bf16[768,64]{1,0:T(8,128)(2,1)}, bf16[768,64]{1,0:T(8,128)(2,1)S(1)}, u32[]{:S(2)}) copy-start(bf16[768,64]{1,0:T(8,128)(2,1)S(1)} %copy.136) | copy-start | bytes 294916
  32.5 546.0 %reduce-scatter.6.cloned.1.call-start = ((), (), s32[]{:S(2)}) async-start(), calls=%async_computation.5 | async-start | bytes 11796480 | tf_op jit(solution)/shard_map/reduce_scatter | solution.py:213
  34.0 203.4 %copy-start.55 = (f32[3072]{0:T(1024)}, f32[3072]{0:T(1024)S(1)}, u32[]{:S(2)}) copy-start(f32[3072]{0:T(1024)S(1)} %add.216) | copy-start | bytes 36868
  232.0 20.5 %copy-start.27 = (f32[512,768]{1,0:T(8,128)}, f32[512,768]{1,0:T(8,128)S(1)}, u32[]{:S(2)}) copy-start(f32[512,768]{1,0:T(8,128)S(1)} %get-tuple-element.409) | copy-start | bytes 4718596
  232.0 20.5 %copy-start.47 = (f32[512]{0:T(512)}, f32[512]{0:T(512)S(1)}, u32[]{:S(2)}) copy-start(f32[512]{0:T(512)S(1)} %broadcast_multiply_fusion.5) | copy-start | bytes 6148
  232.3 20.2 %copy-start.60 = (f32[512]{0:T(512)}, f32[512]{0:T(512)S(1)}, u32[]{:S(2)}) copy-start(f32[512]{0:T(512)S(1)} %add_rsqrt_fusion) | copy-start | bytes 6148
  232.4 16.6 %slice-start = ((s8[14254080]{0:T(1024)(128)(4,1)}), s8[4194304]{0:T(1024)(128)(4,1)S(1)}, s32[]{:S(2)}) async-start(s8[14254080]{0:T(1024)(128)(4,1)} %bitcast.338), calls=%async_computation.9 | async-start | bytes 8388608
  232.4 16.6 %slice-start.1 = ((s8[14254080]{0:T(1024)(128)(4,1)}), s8[4194304]{0:T(1024)(128)(4,1)S(1)}, s32[]{:S(2)}) async-start(s8[14254080]{0:T(1024)(128)(4,1)} %bitcast.338), calls=%async_computation.10 | async-start | bytes 8388608
  237.4 11.5 %copy-start.78 = (f32[512,3072]{1,0:T(8,128)}, f32[512,3072]{1,0:T(8,128)S(1)}, u32[]{:S(2)}) copy-start(f32[512,3072]{1,0:T(8,128)S(1)} %fusion.85) | copy-start | bytes 18874372
  237.4 11.5 %slice-start.2 = ((s8[14254080]{0:T(1024)(128)(4,1)}), s8[4194304]{0:T(1024)(128)(4,1)S(1)}, s32[]{:S(2)}) async-start(s8[14254080]{0:T(1024)(128)(4,1)} %bitcast.338), calls=%async_computation.11 | async-start | bytes 8388608
  237.4 11.5 %slice-start.3 = ((s8[14254080]{0:T(1024)(128)(4,1)}), s8[1671168]{0:T(1024)(128)(4,1)S(1)}, s32[]{:S(2)}) async-start(s8[14254080]{0:T(1024)(128)(4,1)} %bitcast.338), calls=%async_computation.12 | async-start | bytes 3342336
  483.4 409.1 %reduce-scatter.8.cloned.1.call-start = ((), (), s32[]{:S(2)}) async-start(), calls=%async_computation.6 | async-start | bytes 32292864 | tf_op jit(solution)/shard_map/reduce_scatter | solution.py:250
  591.5 6.2 copy-start.38
  592.2 7.7 copy-start.77
  597.7 7.8 slice-start.5
  599.9 5.6 copy-start.41
  611.9 312.3 %reduce-scatter.10.cloned.1.call-start = ((), (), s32[]{:S(2)}) async-start(), calls=%async_computation.8 | async-start | bytes 442368
  621.5 369.6 %all-reduce.2.cloned.1.call-start = ((), (), s32[]{:S(2)}) async-start(), calls=%async_computation.7 | async-start | bytes 3588096 | tf_op jit(solution)/shard_map/psum | solution.py:254
  896.6 9.6 copy-start.39
  906.2 28.8 %copy-start.63 = (f32[96,13]{0,1:T(8,128)S(1)}, f32[96,13]{0,1:T(8,128)}, u32[]{:S(2)}) copy-start(f32[96,13]{0,1:T(8,128)} %param.23) | copy-start | bytes 14980
  906.2 28.8 %copy-start.64 = (f32[96,13]{0,1:T(8,128)S(1)}, f32[96,13]{0,1:T(8,128)}, u32[]{:S(2)}) copy-start(f32[96,13]{0,1:T(8,128)} %param.27) | copy-start | bytes 14980
  906.3 28.8 %copy-start.65 = (f32[96,13]{0,1:T(8,128)S(1)}, f32[96,13]{0,1:T(8,128)}, u32[]{:S(2)}) copy-start(f32[96,13]{0,1:T(8,128)} %param.25) | copy-start | bytes 14980
  906.3 29.4 %copy-start.62 = (f32[96,13]{0,1:T(8,128)S(1)}, f32[96,13]{0,1:T(8,128)}, u32[]{:S(2)}) copy-start(f32[96,13]{0,1:T(8,128)} %param.29) | copy-start | bytes 14980
  935.7 64.4 %copy-start.44 = (f32[96,13]{0,1:T(8,128)}, f32[96,13]{0,1:T(8,128)S(1)}, u32[]{:S(2)}) copy-start(f32[96,13]{0,1:T(8,128)S(1)} %get-tuple-element.378) | copy-start | bytes 14980
  991.1 8.9 copy-start.32
  (71 other events, 170.4 us)
Sparse Core Ops, SparseCore 0:
  19.0 46.6 all-gather.4
  68.2 70.0 all-gather.2
  483.5 95.0 reduce-scatter.5
  612.0 280.4 reduce-scatter.7
  895.2 28.9 reduce-scatter.9
  928.2 62.9 all-reduce.1
where the time goes:
time: 1020 us; the launch traced here: 1010 us
  waiting for transfers between devices  510 us (50%)
  matrix products  282 us (28%)
  local copies, waits for them, and re-layouts  123 us (12%)
  other arithmetic  67.8 us (7%)
  between operations  16.2 us (2%)
    reduce_scatter x1, waiting for transfers between devices, on_device(): lax.psum_scatter(grad_mats, 'grp', scatter_dimension=0, tiled=True)  271 us
    dot_general x120, matrix products, precise(): jnp.dot(left, right, preferred_element_type=jnp.float32, precision=carefu...  171 us
    reduce_scatter x1, waiting for transfers between devices, on_device(): lax.psum_scatter(jnp.concatenate([d_keys_part.reshape(count, 2 * D), d_va...  87.1 us
    all_gather x1, waiting for transfers between devices, on_device(): lax.all_gather(key_feat.reshape(rows, 2 * D), 'seq', axis=0, tiled=True)  67.8 us
    psum x1, waiting for transfers between devices, on_device(): lax.psum(owned_mats.astype(jnp.bfloat16), 'seq').astype(jnp.float32)  54.8 us
    dynamic_update_slice x36, local copies, waits for them, and re-layouts, on_device(): lax.map(attend_back, (query_heads, key_heads, value_major, state_in, tota...  25.7 us
    dynamic_slice x48, local copies, waits for them, and re-layouts, on_device(): lax.map(attend_back, (query_heads, key_heads, value_major, state_in, tota...  23.5 us
    unnamed x173, local copies, waits for them, and re-layouts  23.3 us
  transfers between devices with their start and end apart: 6, of which 6 were waited for; matrix products, arithmetic and copies ran while one was open for 7% of the time, Pallas kernels for 0%

commit v1 on v0

--- a/solution.py
+++ b/solution.py
@@ -122,7 +122,12 @@
     key_feat = key_full.astype(jnp.bfloat16)
     value_heads = values_low.reshape(rows, HEADS, HD)
     gath_keys, gath_values = (
-        lax.all_gather(key_feat.reshape(rows, 2 * D), "seq", axis=0, tiled=True),
+        jnp.concatenate(
+            lax.all_to_all(
+                jnp.stack([key_feat.reshape(rows, 2 * D)] * lax.axis_size("seq")), "seq", 0, 0
+            ),
+            axis=0,
+        ),
         lax.all_gather(values_low, "seq", axis=0, tiled=True),
     )
     positions = jnp.arange(gath_keys.shape[0], dtype=jnp.int32)

time: 1020 us -> 1050 us (1.029)
  local copies, waits for them, and re-layouts: 123 us -> 147 us
    all_to_all x0 -> x1, waiting for transfers between devices: none -> 73.1 us  [on_device(): lax.all_to_all(jnp.stack([key_feat.reshape(rows, 2 * D)] * lax.axis_size(...]
    all_gather x1 -> x0, waiting for transfers between devices: 67.8 us -> none  [on_device(): lax.all_gather(key_feat.reshape(rows, 2 * D), 'seq', axis=0, tiled=True)]
    all_gather x1, waiting for transfers between devices: 12.7 us -> 0.01 us  [on_device(): lax.all_gather(values_low, 'seq', axis=0, tiled=True)]
    reshape x0 -> x1, local copies, waits for them, and re-layouts: none -> 11 us  [on_device(): jnp.concatenate(lax.all_to_all(jnp.stack([key_feat.reshape(rows, 2 * D)]...]
    all_to_all x0 -> x1, local copies, waits for them, and re-layouts: none -> 10.5 us  [on_device(): lax.all_to_all(jnp.stack([key_feat.reshape(rows, 2 * D)] * lax.axis_size(...]
    unnamed x173 -> x169, local copies, waits for them, and re-layouts: 23.3 us -> 22.7 us
  transfers between devices with their start and end apart: 6 -> 6, of which waited for: 6 -> 5; matrix products, arithmetic and copies ran while one was open for 7% -> 7% of each run, Pallas kernels for 0% -> 0%
where the time goes in v1:
time: 1050 us; the launch traced here: 1030 us
  waiting for transfers between devices  503 us (48%)
  matrix products  286 us (27%)
  local copies, waits for them, and re-layouts  147 us (14%)
  other arithmetic  66.1 us (6%)
  between operations  15.9 us (2%)
    reduce_scatter x1, waiting for transfers between devices, on_device(): lax.psum_scatter(grad_mats, 'grp', scatter_dimension=0, tiled=True)  271 us
    dot_general x120, matrix products, precise(): jnp.dot(left, right, preferred_element_type=jnp.float32, precision=carefu...  170 us
    reduce_scatter x1, waiting for transfers between devices, on_device(): lax.psum_scatter(jnp.concatenate([d_keys_part.reshape(count, 2 * D), d_va...  87.5 us
    all_to_all x1, waiting for transfers between devices, on_device(): lax.all_to_all(jnp.stack([key_feat.reshape(rows, 2 * D)] * lax.axis_size(...  73.1 us
    psum x1, waiting for transfers between devices, on_device(): lax.psum(owned_mats.astype(jnp.bfloat16), 'seq').astype(jnp.float32)  54.8 us
    dynamic_update_slice x36, local copies, waits for them, and re-layouts, on_device(): lax.map(attend_back, (query_heads, key_heads, value_major, state_in, tota...  25.7 us
    dynamic_slice x48, local copies, waits for them, and re-layouts, on_device(): lax.map(attend_back, (query_heads, key_heads, value_major, state_in, tota...  23.5 us
    unnamed x169, local copies, waits for them, and re-layouts  22.7 us
  transfers between devices with their start and end apart: 6, of which 5 were waited for; matrix products, arithmetic and copies ran while one was open for 7% of the time, Pallas kernels for 0%

profile of v1, /device:TPU:0, one launch (start us, length us, event | category | flops | bytes accessed | tf_op | source)
XLA Modules:
  0.0 1034.5 jit_solution(14767387564600683333)
XLA Ops:
  11.7 4.2 convolution_add_fusion.3
  28.2 3.2 stack.21
  31.4 5.2 all-to-all-start
  53.2 2.7 copy.82
  60.2 73.1 %all-to-all-done = bf16[4,512,1536]{1,2,0:T(8,128)(2,1)} async-done(((bf16[4,512,1536]{1,2,0:T(8,128)(2,1)}), bf16[4,512,1536]{1,2,0:T(8,128)(2,1)}, u32[]{:S(2)}, u32[]{:S(2)}) %all-to-all-start) | async-done | bytes 6291488 | tf_op jit(solution)/shard_map/all_to_all | solution.py:126
  133.3 10.5 %copy.79 = bf16[4,512,1536]{1,0,2:T(4,128)(2,1)} copy(bf16[4,512,1536]{1,2,0:T(8,128)(2,1)} %all-to-all-done) | data formatting | bytes 12582912 | tf_op jit(solution)/shard_map/all_to_all | solution.py:126
  143.8 11.0 %reshape.287 = bf16[2048,12,128]{0,2,1:T(8,128)(2,1)} reshape(bf16[4,512,1536]{1,0,2:T(4,128)(2,1)} %copy.79) | data formatting | bytes 12582912 | tf_op jit(solution)/shard_map/reshape | solution.py:125
  154.9 4.6 copy.80
  159.5 5.5 fusion.79
  165.0 4.7 convert_reduce_fusion
  171.0 81.3 %while.33 = (s32[]{:T(128)}, f32[12,512,64]{1,2,0:T(8,128)}, f32[12,512]{1,0:T(8,128)}, bf16[12,512,128]{2,1,0:T(8,128)(2,1)}, bf16[12,512,128]{2,1,0:T(8,128)(2...) while((s32[]{:T(128)}, f32[12,512,64]{1,2,0:T(8,128)}, ...), condition=%wide.region_13.14_spmd.clone, body=%wide.region_11.13_spmd.clone.sunk | while | flops 194183168 | bytes 3231861 | solution.py:157
  257.0 5.0 fusion.87
  262.1 11.5 %convert_reduce_fusion.1 = (f32[3072]{0:T(1024)}, bf16[512,3072]{1,0:T(8,128)(2,1)S(1)}) fusion(f32[512,3072]{1,0:T(8,128)S(1)} %fusion.87, f32[3072]{0:T(1024)S(1)} %add.221, bf16[512,768]{1,0:T(8,128)(2,1)S(1)} %copy-done.38, bf16[768,9280]{0,1:T(8,128)(2,1)} %param.20), kind=kOutput, calls=%fused_computation.105 | convolution fusion | flops 2452091904 | bytes 14966784 | tf_op jit(solution)/shard_map/dot_general | solution.py:170
  273.6 3.5 multiply_reduce_fusion
  283.2 202.2 %while.34 = (s32[]{:T(128)}, f32[12,512,128]{1,2,0:T(8,128)}, f32[12,512,128]{1,2,0:T(8,128)}, f32[12,512,64]{1,2,0:T(8,128)}, f32[12,128,64]{1,2,0:T(8,128)}, /...) while((s32[]{:T(128)}, f32[12,512,128]{1,2,0:T(8,128)}, ...), condition=%wide.region_20.21_spmd.clone.clone, body=%wide.region_18.20_spmd.clone.clone.sunk | while | flops 723526784 | bytes 10363109 | solution.py:202
  485.5 5.1 multiply_convert_fusion.1
  490.6 5.4 multiply_convert_fusion
  496.0 11.6 %pad_maximum_fusion = bf16[2048,2304]{0,1:T(8,128)(2,1)} fusion(bf16[2048,768]{0,1:T(8,128)(2,1)S(1)} %bitcast.305, bf16[2048,1536]{0,1:T(8,128)(2,1)S(1)} %bitcast.300), kind=kLoop, calls=%fused_computation.92 | loop fusion | flops 18874368 | bytes 18874368 | tf_op jit(solution)/shard_map/concatenate | solution.py:219
  509.0 3.4 multiply_reduce_fusion.4
  515.7 87.5 %reduce-scatter.6.cloned.1.call-done = bf16[512,2304]{0,1:T(8,128)(2,1)} async-done(((bf16[2048,2304]{0,1:T(8,128)(2,1)}), bf16[512,2304]{0,1:T(8,128)(2,1)}) %reduce-scatter.6.cloned.1.call-update) | async-done | bytes 2359312 | tf_op jit(solution)/shard_map/reduce_scatter | solution.py:218
  616.8 5.4 convolution_dynamic-update-slice_fusion
  624.6 5.5 convolution_dynamic-update-slice_fusion.1
  630.2 5.5 bitcast_dynamic-update-slice_fusion
  639.1 6.0 fusion.113
  646.5 270.7 %reduce-scatter.8.cloned.1.call-done = f32[96,9280]{1,0:T(8,128)} async-done(((f32[768,9280]{1,0:T(8,128)}), f32[96,9280]{1,0:T(8,128)}) %reduce-scatter.8.cloned.1.call-update) | async-done | bytes 3563536 | tf_op jit(solution)/shard_map/reduce_scatter | solution.py:255
  917.2 3.4 convert_element_type.151
  921.3 9.6 add_convert_fusion
  932.4 16.5 %reduce-scatter.10.cloned.1.call-done = f32[96,13]{1,0:T(8,128)} async-done(((f32[768,13]{1,0:T(8,128)}), f32[96,13]{1,0:T(8,128)}) %reduce-scatter.10.cloned.1.call-update) | async-done | bytes 5008
  949.8 9.9 psum.15
  961.0 54.8 %all-reduce.2.cloned.1.call-done = bf16[96,9280]{1,0:T(8,128)(2,1)} async-done(((bf16[96,9280]{1,0:T(8,128)(2,1)}), bf16[96,9280]{1,0:T(8,128)(2,1)}) %all-reduce.2.cloned.1.call-update) | async-done | bytes 1781776 | tf_op jit(solution)/shard_map/psum | solution.py:259
  1015.8 8.9 fusion.166
  1024.8 2.7 multiply_add_fusion.1
  (575 shorter events, 360.9 us)
Async XLA Ops:
  8.7 7.3 copy-start.51
  8.7 7.3 copy-start.69
  8.7 248.3 %copy-start.67 = (f32[768]{0:T(1024)}, f32[768]{0:T(1024)S(1)}, u32[]{:S(2)}) copy-start(f32[768]{0:T(1024)S(1)} %get-tuple-element.327) | copy-start | bytes 9220
  8.7 268.4 %copy-start.49 = (f32[768]{0:T(1024)}, f32[768]{0:T(1024)S(1)}, u32[]{:S(2)}) copy-start(f32[768]{0:T(1024)S(1)} %get-tuple-element.325) | copy-start | bytes 9220
  10.0 6.0 copy-start.43
  11.7 33.2 %copy-start.28 = (bf16[768,64]{1,0:T(8,128)(2,1)}, bf16[768,64]{1,0:T(8,128)(2,1)S(1)}, u32[]{:S(2)}) copy-start(bf16[768,64]{1,0:T(8,128)(2,1)S(1)} %copy.138) | copy-start | bytes 294916
  31.4 102.0 %all-to-all-start = ((bf16[4,512,1536]{1,2,0:T(8,128)(2,1)}), bf16[4,512,1536]{1,2,0:T(8,128)(2,1)}, u32[]{:S(2)}, u32[]{:S(2)}) async-start(bf16[4,512,1536]{1,2,0:T(8,128)(2,1)} %stack.21), calls=%async_computation | async-start | bytes 12582912 | tf_op jit(solution)/shard_map/all_to_all | solution.py:126
  36.6 118.3 %all-gather.2.cloned.1.call-start = ((), (), s32[]{:S(2)}) async-start(), calls=%async_computation.4 | async-start | bytes 3932160 | tf_op jit(solution)/shard_map/all_gather | solution.py:131
  39.0 564.1 %reduce-scatter.6.cloned.1.call-start = ((), (), s32[]{:S(2)}) async-start(), calls=%async_computation.5 | async-start | bytes 11796480 | tf_op jit(solution)/shard_map/reduce_scatter | solution.py:218
  41.5 220.5 %copy-start.53 = (f32[3072]{0:T(1024)}, f32[3072]{0:T(1024)S(1)}, u32[]{:S(2)}) copy-start(f32[3072]{0:T(1024)S(1)} %add.221) | copy-start | bytes 36868
  256.6 20.5 %copy-start.25 = (f32[512,768]{1,0:T(8,128)}, f32[512,768]{1,0:T(8,128)S(1)}, u32[]{:S(2)}) copy-start(f32[512,768]{1,0:T(8,128)S(1)} %get-tuple-element.407) | copy-start | bytes 4718596
  256.6 20.5 %copy-start.45 = (f32[512]{0:T(512)}, f32[512]{0:T(512)S(1)}, u32[]{:S(2)}) copy-start(f32[512]{0:T(512)S(1)} %broadcast_multiply_fusion.4) | copy-start | bytes 6148
  256.9 20.2 %copy-start.58 = (f32[512]{0:T(512)}, f32[512]{0:T(512)S(1)}, u32[]{:S(2)}) copy-start(f32[512]{0:T(512)S(1)} %add_rsqrt_fusion) | copy-start | bytes 6148
  257.0 16.6 %slice-start = ((s8[14254080]{0:T(1024)(128)(4,1)}), s8[4194304]{0:T(1024)(128)(4,1)S(1)}, s32[]{:S(2)}) async-start(s8[14254080]{0:T(1024)(128)(4,1)} %bitcast.336), calls=%async_computation.9 | async-start | bytes 8388608
  257.0 16.6 %slice-start.1 = ((s8[14254080]{0:T(1024)(128)(4,1)}), s8[4194304]{0:T(1024)(128)(4,1)S(1)}, s32[]{:S(2)}) async-start(s8[14254080]{0:T(1024)(128)(4,1)} %bitcast.336), calls=%async_computation.10 | async-start | bytes 8388608
  262.0 11.5 %copy-start.76 = (f32[512,3072]{1,0:T(8,128)}, f32[512,3072]{1,0:T(8,128)S(1)}, u32[]{:S(2)}) copy-start(f32[512,3072]{1,0:T(8,128)S(1)} %fusion.87) | copy-start | bytes 18874372
  262.0 11.5 %slice-start.2 = ((s8[14254080]{0:T(1024)(128)(4,1)}), s8[4194304]{0:T(1024)(128)(4,1)S(1)}, s32[]{:S(2)}) async-start(s8[14254080]{0:T(1024)(128)(4,1)} %bitcast.336), calls=%async_computation.11 | async-start | bytes 8388608
  262.0 11.5 %slice-start.3 = ((s8[14254080]{0:T(1024)(128)(4,1)}), s8[1671168]{0:T(1024)(128)(4,1)S(1)}, s32[]{:S(2)}) async-start(s8[14254080]{0:T(1024)(128)(4,1)} %bitcast.336), calls=%async_computation.12 | async-start | bytes 3342336
  507.6 409.6 %reduce-scatter.8.cloned.1.call-start = ((), (), s32[]{:S(2)}) async-start(), calls=%async_computation.6 | async-start | bytes 32292864 | tf_op jit(solution)/shard_map/reduce_scatter | solution.py:255
  616.1 6.2 copy-start.36
  616.8 7.8 copy-start.75
  622.3 7.9 slice-start.5
  624.6 5.6 copy-start.39
  636.6 312.4 %reduce-scatter.10.cloned.1.call-start = ((), (), s32[]{:S(2)}) async-start(), calls=%async_computation.8 | async-start | bytes 442368
  646.2 369.6 %all-reduce.2.cloned.1.call-start = ((), (), s32[]{:S(2)}) async-start(), calls=%async_computation.7 | async-start | bytes 3588096 | tf_op jit(solution)/shard_map/psum | solution.py:259
  921.3 9.6 copy-start.37
  930.9 28.8 %copy-start.61 = (f32[96,13]{0,1:T(8,128)S(1)}, f32[96,13]{0,1:T(8,128)}, u32[]{:S(2)}) copy-start(f32[96,13]{0,1:T(8,128)} %param.23) | copy-start | bytes 14980
  930.9 28.8 %copy-start.62 = (f32[96,13]{0,1:T(8,128)S(1)}, f32[96,13]{0,1:T(8,128)}, u32[]{:S(2)}) copy-start(f32[96,13]{0,1:T(8,128)} %param.27) | copy-start | bytes 14980
  930.9 28.8 %copy-start.63 = (f32[96,13]{0,1:T(8,128)S(1)}, f32[96,13]{0,1:T(8,128)}, u32[]{:S(2)}) copy-start(f32[96,13]{0,1:T(8,128)} %param.25) | copy-start | bytes 14980
  930.9 29.4 %copy-start.60 = (f32[96,13]{0,1:T(8,128)S(1)}, f32[96,13]{0,1:T(8,128)}, u32[]{:S(2)}) copy-start(f32[96,13]{0,1:T(8,128)} %param.29) | copy-start | bytes 14980
  960.4 64.4 %copy-start.42 = (f32[96,13]{0,1:T(8,128)}, f32[96,13]{0,1:T(8,128)S(1)}, u32[]{:S(2)}) copy-start(f32[96,13]{0,1:T(8,128)S(1)} %get-tuple-element.378) | copy-start | bytes 14980
  1015.8 8.9 copy-start.30
  (69 other events, 166.9 us)
Sparse Core Ops, SparseCore 0:
  39.8 93.1 all-gather.1
  507.7 95.4 reduce-scatter.5
  636.7 280.4 reduce-scatter.7
  919.8 29.0 reduce-scatter.9
  952.9 62.8 all-reduce.1
